TPU v7x, 128 devices: a whole 4x4x4 slice. The times are simulated.
128 devices in a mesh: gx: 16 (over x, y), gy: 8 (over z, core).
Axes of the slice: x: 4, y: 4, z: 4, core: 2. Of those that a mesh axis runs over, the one named last changes fastest.
Arguments:
- height_start: float32 [32, 2048, 1024], P(None, 'gx', 'gy'), may hold values from -6 to 6
- flow_x_start: float32 [32, 2048, 1024], P(None, 'gx', 'gy'), may hold values from -6 to 6
- flow_y_start: float32 [32, 2048, 1024], P(None, 'gx', 'gy'), may hold values from -6 to 6
- depth_field: float32 [2048, 1024], P('gx', 'gy'), may hold values from 0.2 to 1.2
- misfit_rows: float32 [32768, 128], P(('gx', 'gy')), may hold values from -6 to 6
- tile_list: int32 [32768, 1], P(('gx', 'gy')), may hold values from 0 to 127; in each aligned block of 256 rows (0 to 255, 256 to 511, ...) at most 4 rows name the same one
- member_list: int32 [32768], P(('gx', 'gy')), may hold values from 0 to 31
- cell_list: int32 [32768], P(('gx', 'gy')), may hold values from 0 to 16383
- count_list: int32 [32768], P(('gx', 'gy')), may hold values from 1 to 128
Outputs:
- height_adjoint: float32 [32, 2048, 1024], P(None, 'gx', 'gy')
- flow_x_adjoint: float32 [32, 2048, 1024], P(None, 'gx', 'gy')
- flow_y_adjoint: float32 [32, 2048, 1024], P(None, 'gx', 'gy')
Inputs may be any that keep to these rules, and one draw needn't show every extreme that they name: `tile_list`: among the records of one device no tile is named more than 4 times.
All inputs are finite; a program needn't handle non-finite values.
Results may differ from a plain program's by a relative error of at most 0.00002.
Values sent between devices are 32-bit elements; how exact they have to be, the bound alone decides.
A program may use at most 128 MiB of HBM per device.

v0:
```python
import jax
import jax.numpy as jnp
from jax import lax
from jax.sharding import PartitionSpec as P

WINDOWS = 4
SUB = 8
STEPS = 32


def shifted(value, axis, steps):
    count = lax.axis_size(axis)
    leading, last = (max(0, -steps), min(count, count - steps))
    return lax.ppermute(value, axis, [(source, source + steps) for source in range(leading, last)])


def window_sums(rows, counts):
    samples = rows.shape[1]
    sample_pos = jnp.arange(samples, dtype=jnp.int32)
    live = sample_pos[None, :] < counts[:, None]
    masked = jnp.where(live, rows, jnp.zeros_like(rows))
    return jnp.sum(masked.reshape(rows.shape[0], STEPS, samples // STEPS), axis=2)


def local(
    height_start,
    flow_x_start,
    flow_y_start,
    depth_field,
    misfit_rows,
    tile_list,
    member_list,
    cell_list,
    count_list,
):
    records = misfit_rows.shape[0]
    devices = lax.axis_size(("gx", "gy"))
    capacity = max(2, 2 * records // devices)
    targets = tile_list[:, 0]
    onehot = (targets[:, None] == jnp.arange(devices, dtype=jnp.int32)[None, :]).astype(jnp.int32)
    earlier = jnp.cumsum(onehot, axis=0) - onehot
    rank_in = jnp.sum(earlier * onehot, axis=1)
    slot_pos = targets * capacity + rank_in
    rows_out = (
        jnp.zeros((devices * capacity, misfit_rows.shape[1]), jnp.float32)
        .at[slot_pos]
        .set(misfit_rows)
    )
    labels = jnp.stack([member_list, cell_list, count_list], axis=1)
    labels_out = jnp.zeros((devices * capacity, 3), jnp.int32).at[slot_pos].set(labels)
    rows_in, labels_in = (
        lax.all_to_all(rows_out, ("gx", "gy"), split_axis=0, concat_axis=0, tiled=True),
        lax.all_to_all(labels_out, ("gx", "gy"), split_axis=0, concat_axis=0, tiled=True),
    )
    increments = window_sums(rows_in, labels_in[:, 2])
    members, tile_rows, tile_cols = height_start.shape
    flat_index = labels_in[:, 0] * (tile_rows * tile_cols) + labels_in[:, 1]
    depth = depth_field[None, :, :]

    def advance(step, state):
        height, flow_x, flow_y = state
        amounts = lax.dynamic_index_in_dim(increments, step, 1, keepdims=False)
        height = height.reshape(-1).at[flat_index].add(amounts).reshape(height.shape)
        rim_x = shifted(height[:, 0:1, :], "gx", -1)
        rim_y = shifted(height[:, :, 0:1], "gy", -1)
        next_x = jnp.concatenate([height[:, 1:, :], rim_x], axis=1)
        next_y = jnp.concatenate([height[:, :, 1:], rim_y], axis=2)
        flow_x = flow_x - 0.6 * (next_x - height)
        flow_y = flow_y - 0.6 * (next_y - height)
        flux_x = depth * flow_x
        flux_y = depth * flow_y
        back_x = shifted(flux_x[:, -1:, :], "gx", 1)
        back_y = shifted(flux_y[:, :, -1:], "gy", 1)
        prev_x = jnp.concatenate([back_x, flux_x[:, :-1, :]], axis=1)
        prev_y = jnp.concatenate([back_y, flux_y[:, :, :-1]], axis=2)
        height = height - 0.6 * (flux_x - prev_x + (flux_y - prev_y))
        return (height, flow_x, flow_y)

    state = (height_start, flow_x_start, flow_y_start)
    for window in range(WINDOWS):
        state = lax.fori_loop(window * SUB, (window + 1) * SUB, advance, state)
    return (state[0], state[1], state[2])


def solution(mesh):
    in_specs = (
        P(None, "gx", "gy"),
        P(None, "gx", "gy"),
        P(None, "gx", "gy"),
        P("gx", "gy"),
        P(("gx", "gy"), None),
        P(("gx", "gy"), None),
        P(("gx", "gy")),
        P(("gx", "gy")),
        P(("gx", "gy")),
    )
    out_specs = (P(None, "gx", "gy"), P(None, "gx", "gy"), P(None, "gx", "gy"))
    return jax.shard_map(local, mesh=mesh, in_specs=in_specs, out_specs=out_specs, check_vma=False)
```

profile of v0, /device:TPU:24, one launch (start us, length us, event | category | flops | bytes accessed | tf_op | source)
XLA Modules:
  0.0 1549.5 jit_solution(17842889030405364449)
XLA Ops:
  9.5 10.3 all-to-all-start
  22.0 7.2 all-to-all-done
  29.1 6.6 all-to-all-start.1
  35.9 9.0 all-to-all-done.1
  45.0 10.2 all_to_all.21
  55.1 6.6 select_reduce_fusion
  61.8 370.1 %while.74 = (s32[]{:T(128)}, f32[32,128,128]{2,1,0:T(8,128)S(1)}, f32[32,128,128]{2,1,0:T(8,128)}, f32[32,128,128]{2,1,0:T(8,128)}, s32[512]{0:T(512)S(1)}, /*in...) while((s32[]{:T(128)}, f32[32,128,128]{2,1,0:T(8,128)S(1)}, f32[32,128,128]{2,1,0:T(8,128)}, ...), condition=%wide.region_8.9_spmd, body=%wide.region_6.8_spmd.sunk | while | flops 9963522 | bytes 48808212 | solution.py:81
  76.1 8.5 broadcast_multiply_fusion.12
  101.0 6.0 fusion.50
  120.9 8.5 broadcast_multiply_fusion.12
  147.1 6.0 fusion.50
  167.0 8.5 broadcast_multiply_fusion.12
  213.4 8.5 broadcast_multiply_fusion.12
  259.9 8.5 broadcast_multiply_fusion.12
  306.3 8.5 broadcast_multiply_fusion.12
  352.8 8.5 broadcast_multiply_fusion.12
  399.3 8.5 broadcast_multiply_fusion.12
  431.9 372.2 %while.75 = (s32[]{:T(128)}, f32[32,128,128]{2,1,0:T(8,128)S(1)}, f32[32,128,128]{2,1,0:T(8,128)}, f32[32,128,128]{2,1,0:T(8,128)}, s32[512]{0:T(512)S(1)}, /*in...) while((s32[]{:T(128)}, f32[32,128,128]{2,1,0:T(8,128)S(1)}, ...), condition=%wide.region_11.12_spmd, body=%wide.region_9.11_spmd.sunk | while | flops 9963526 | bytes 48808280 | solution.py:81
  446.3 8.5 broadcast_multiply_fusion.13
  492.7 8.5 broadcast_multiply_fusion.13
  539.2 8.5 broadcast_multiply_fusion.13
  565.7 6.0 fusion.51
  585.6 8.5 broadcast_multiply_fusion.13
  632.1 8.5 broadcast_multiply_fusion.13
  678.6 8.5 broadcast_multiply_fusion.13
  725.0 8.5 broadcast_multiply_fusion.13
  771.5 8.5 broadcast_multiply_fusion.13
  804.1 371.9 %while.76 = (s32[]{:T(128)}, f32[32,128,128]{2,1,0:T(8,128)S(1)}, f32[32,128,128]{2,1,0:T(8,128)}, f32[32,128,128]{2,1,0:T(8,128)}, s32[512]{0:T(512)S(1)}, /*in...) while((s32[]{:T(128)}, f32[32,128,128]{2,1,0:T(8,128)S(1)}, ...), condition=%wide.region_14.15_spmd, body=%wide.region_12.14_spmd.sunk | while | flops 9963526 | bytes 48808280 | solution.py:81
  818.2 8.5 broadcast_multiply_fusion.14
  864.6 8.5 broadcast_multiply_fusion.14
  911.1 8.5 broadcast_multiply_fusion.14
  957.5 8.5 broadcast_multiply_fusion.14
  1004.0 8.5 broadcast_multiply_fusion.14
  1050.5 8.5 broadcast_multiply_fusion.14
  1077.0 6.0 fusion.52
  1096.9 8.5 broadcast_multiply_fusion.14
  1143.4 8.5 broadcast_multiply_fusion.14
  1176.0 371.9 %while.77 = (s32[]{:T(128)}, f32[32,128,128]{2,1,0:T(8,128)S(1)}, f32[32,128,128]{2,1,0:T(8,128)}, f32[32,128,128]{2,1,0:T(8,128)}, s32[512]{0:T(512)S(1)}, /*in...) while((s32[]{:T(128)}, f32[32,128,128]{2,1,0:T(8,128)S(1)}, ...), condition=%wide.region_17.18_spmd, body=%wide.region_15.17_spmd.sunk | while | flops 9963526 | bytes 48808280 | solution.py:81
  1190.1 8.5 broadcast_multiply_fusion.15
  1236.6 8.5 broadcast_multiply_fusion.15
  1263.1 6.0 fusion.53
  1283.0 8.5 broadcast_multiply_fusion.15
  1329.5 8.5 broadcast_multiply_fusion.15
  1376.0 8.5 broadcast_multiply_fusion.15
  1422.4 8.5 broadcast_multiply_fusion.15
  1468.9 8.5 broadcast_multiply_fusion.15
  1515.3 8.5 broadcast_multiply_fusion.15
  1541.9 6.0 fusion.53
  (770 shorter events, 1184.8 us)
Async XLA Ops:
  9.5 19.6 %all-to-all-start = ((s32[128,4,3]{1,2,0:T(4,128)}), s32[128,4,3]{1,2,0:T(4,128)S(1)}, u32[]{:S(2)}, u32[]{:S(2)}) async-start(s32[128,4,3]{1,2,0:T(4,128)} %copy.56), calls=%async_computation | async-start | bytes 524288 | tf_op jit(solution)/shard_map/all_to_all | solution.py:53
  29.1 15.8 %all-to-all-start.1 = ((f32[128,4,128]{2,1,0:T(4,128)}), f32[128,4,128]{2,1,0:T(4,128)S(1)}, u32[]{:S(2)}, u32[]{:S(2)}) async-start(f32[128,4,128]{2,1,0:T(4,128)} %bitcast.37), calls=%async_computation.1 | async-start | bytes 524288 | tf_op jit(solution)/shard_map/all_to_all | solution.py:52
  67.9 8.2 collective-permute-start.1
  90.1 8.9 collective-permute-start.3
  134.9 10.2 collective-permute-start.3
  139.3 7.7 collective-permute-start.2
  180.9 10.6 collective-permute-start.3
  227.4 10.6 collective-permute-start.3
  232.2 7.7 collective-permute-start.2
  273.9 10.6 collective-permute-start.3
  278.7 7.7 collective-permute-start.2
  320.3 10.6 collective-permute-start.3
  366.8 10.6 collective-permute-start.3
  413.2 10.6 collective-permute-start.3
  418.1 7.7 collective-permute-start.2
  460.2 10.6 collective-permute-start.7
  465.1 7.7 collective-permute-start.6
  506.7 10.6 collective-permute-start.7
  511.5 7.7 collective-permute-start.6
  553.2 10.6 collective-permute-start.7
  599.6 10.6 collective-permute-start.7
  646.1 10.6 collective-permute-start.7
  692.6 10.6 collective-permute-start.7
  697.4 7.7 collective-permute-start.6
  739.0 10.6 collective-permute-start.7
  743.9 7.7 collective-permute-start.6
  785.5 10.6 collective-permute-start.7
  790.3 7.7 collective-permute-start.6
  832.1 10.6 collective-permute-start.11
  878.6 10.6 collective-permute-start.11
  883.4 7.7 collective-permute-start.10
  925.1 10.6 collective-permute-start.11
  929.9 7.7 collective-permute-start.10
  971.5 10.6 collective-permute-start.11
  976.4 7.7 collective-permute-start.10
  1018.0 10.6 collective-permute-start.11
  1064.5 10.6 collective-permute-start.11
  1110.9 10.6 collective-permute-start.11
  1157.4 10.6 collective-permute-start.11
  1204.1 10.6 collective-permute-start.15
  1250.5 10.6 collective-permute-start.15
  1297.0 10.6 collective-permute-start.15
  1343.5 10.6 collective-permute-start.15
  1389.9 10.6 collective-permute-start.15
  1394.8 7.7 collective-permute-start.14
  1436.4 10.6 collective-permute-start.15
  1482.9 10.6 collective-permute-start.15
  1529.3 10.6 collective-permute-start.15
  (123 other events, 670.5 us)
where the time goes:
time: 1560 us; the launch traced here: 1550 us
  other arithmetic  605 us (39%)
  local copies, waits for them, and re-layouts  484 us (31%)
  starting transfers between devices  427 us (27%)
  waiting for transfers between devices  28.2 us (2%)
    ppermute x128, starting transfers between devices, shifted(): lax.ppermute(value, axis, [(source, source + steps) for source in range(l...  410 us
    mul x32, other arithmetic, advance(): flux_y = depth * flow_y  273 us
    sub x32, other arithmetic, advance(): height = height - 0.6 * (flux_x - prev_x + (flux_y - prev_y))  193 us
    slice x64, local copies, waits for them, and re-layouts, advance(): back_y = shifted(flux_y[:, :, -1:], 'gy', 1)  132 us
    scatter-add x32, other arithmetic, advance(): height.reshape(-1).at[flat_index].add(amounts).reshape(height.shape)  131 us
    ppermute x64, local copies, waits for them, and re-layouts, shifted(): lax.ppermute(value, axis, [(source, source + steps) for source in range(l...  126 us
    slice x32, local copies, waits for them, and re-layouts, advance(): next_y = jnp.concatenate([height[:, :, 1:], rim_y], axis=2)  61.7 us
    slice x32, local copies, waits for them, and re-layouts, advance(): next_x = jnp.concatenate([height[:, 1:, :], rim_x], axis=1)  48.8 us
  transfers between devices with their start and end apart: 130, of which 33 were waited for; matrix products, arithmetic and copies ran while one was open for 17% of the time, Pallas kernels for 0%

commit v1 on v0

v1 whole, which is shorter than its diff:
```python
import jax
import jax.numpy as jnp
from jax import lax
from jax.experimental import pallas as pl
from jax.experimental.pallas import tpu as pltpu
from jax.sharding import PartitionSpec as P

MESH = pl.DeviceIdType.MESH
F32 = jnp.float32
BF16 = jnp.bfloat16
STEPS = 32
EVENTS = 32
TILE = 128
GROUPS = 4
XI = 32
YI = 16
PY = YI + 1
SLOTS = 4
CELLS = TILE * TILE * EVENTS // 128


def three(x):
    high = x.astype(BF16)
    rest = x - high.astype(F32)
    mid = rest.astype(BF16)
    low = (rest - mid.astype(F32)).astype(BF16)
    return high, mid, low


def dot(a, b):
    return jnp.dot(a, b, preferred_element_type=F32)


def iota(shape, axis):
    return lax.broadcasted_iota(jnp.int32, shape, axis)


def slot_kernel(rows_ref, meta_ref, out_ref):
    records = rows_ref.shape[0]
    tile, member, cell, count = (meta_ref[i : i + 1, :] for i in range(4))
    hit = tile == iota((128, records), 0)
    earlier_mask = jnp.where(iota((records, records), 0) < iota((records, records), 1), 1.0, 0.0)
    rank = dot(jnp.where(hit, 1.0, 0.0).astype(BF16), earlier_mask.astype(BF16)).astype(jnp.int32)
    x, y = cell // TILE, cell % TILE
    vector_row = ((x % XI) * TILE + (y % YI) * 8 + y // YI).astype(F32)
    lane_of = ((x // XI) * EVENTS + member).astype(F32)
    countf = count.astype(F32)
    parts = three(rows_ref[...])
    lane = iota((128, 128), 1)
    total = jnp.zeros((128, 128), F32)
    ids = jnp.full((128, 128), -1.0, F32)
    for j in range(SLOTS):
        sel = hit & (rank == j)
        pick = jnp.where(sel, 1.0, 0.0).astype(BF16)
        found = dot(pick, parts[0]) + dot(pick, parts[1]) + dot(pick, parts[2])

        def of(value):
            return jnp.sum(jnp.where(sel, value, 0.0), axis=1, keepdims=True)

        found = jnp.where(lane.astype(F32) < of(countf), found, 0.0)
        window = jnp.where(iota((128, 128), 0) // 4 + STEPS * j == lane, 1.0, 0.0).astype(BF16)
        a, b, c = three(found)
        total = total + (dot(a, window) + dot(b, window) + dot(c, window))
        ids = jnp.where(lane == j, of(vector_row + 1.0) - 1.0, ids)
        ids = jnp.where(lane == SLOTS + j, of(lane_of + 1.0) - 1.0, ids)
    out_ref[:, 0:128] = total
    out_ref[:, 128:256] = ids


def sweep_kernel(
    p_in, q_in, r_in, depth_ref, slots_ref, p_out, q_out, r_out,
    stage, p2, wf, vf, cf, inj, onehot, rhs, lanes_of, inc,
    send_buf, recv_buf, init_send, init_recv, wh, ch, vh, chy,
    in_sem, out_sem, send_sem, recv_sem, init_send_sem, init_recv_sem,
):
    gx, gy = lax.axis_index("gx"), lax.axis_index("gy")
    nx, ny = lax.axis_size("gx"), lax.axis_size("gy")
    target = [(gx + 1, gy), (gx - 1, gy), (gx, gy + 1), (gx, gy - 1)]
    sends = [gx < nx - 1, gx > 0, gy < ny - 1, gy > 0]
    receives = [sends[1], sends[0], sends[3], sends[2]]

    loads = [
        pltpu.make_async_copy(src, stage.at[i], in_sem.at[i])
        for i, src in enumerate((p_in, q_in, r_in))
    ]
    for copy in loads:
        copy.start()
    recv_buf[...] = jnp.zeros_like(recv_buf)
    init_recv[...] = jnp.zeros_like(init_recv)

    barrier = pltpu.get_barrier_semaphore()
    for d in range(4):

        @pl.when(sends[d])
        def _():
            pl.semaphore_signal(barrier, inc=1, device_id=target[d], device_id_type=MESH)

    pl.semaphore_wait(barrier, sum(jnp.where(peer, 1, 0) for peer in sends))

    def edge_copy(d, slot):
        return pltpu.make_async_remote_copy(
            src_ref=send_buf.at[d, slot],
            dst_ref=recv_buf.at[d, slot],
            send_sem=send_sem.at[d, slot],
            recv_sem=recv_sem.at[d, slot],
            device_id=target[d],
            device_id_type=MESH,
        )

    def init_copy(i):
        return pltpu.make_async_remote_copy(
            src_ref=init_send.at[i],
            dst_ref=init_recv.at[i],
            send_sem=init_send_sem.at[i],
            recv_sem=init_recv_sem.at[i],
            device_id=target[2 * i],
            device_id_type=MESH,
        )

    lane = iota((8, 128), 1)
    sub = iota((8, 128), 0)
    group = lane // EVENTS

    def tile(ref, row):
        return ref[pl.ds(pl.multiple_of(row, 8), 8), :]

    def put(ref, row, value):
        ref[pl.ds(pl.multiple_of(row, 8), 8), :] = value

    def p_row(x, y):
        return (x * PY + y) * 8

    def w_row(x, y):
        return ((x + 1) * YI + y) * 8

    def v_row(x, y):
        return (x * PY + y + 1) * 8

    def c_row(x, y):
        return (x * YI + y) * 8

    def pack_x(load, source):
        packed = []
        for j in range(4):
            total = None
            for g in range(GROUPS):
                value = load(4 * j + g)
                shift = ((g - source) * EVENTS) % 128
                if shift:
                    value = pltpu.roll(value, shift, axis=1)
                total = value if total is None else jnp.where(group == g, value, total)
            packed.append(total)
        return packed

    def unpack_x(ref, y, to):
        value = ref[pl.ds((y // 4) * 8, 8), :]
        shift = ((to - y % 4) * EVENTS) % 128
        return pltpu.roll(value, shift, axis=1) if shift else value

    inc[...] = slots_ref[:, 0:128]
    ids = slots_ref[:, 128:256]
    rows_of = ids.T
    for j in range(SLOTS):
        lanes_of[pl.ds(j * 128, 128), :] = jnp.broadcast_to(ids[:, SLOTS + j : SLOTS + j + 1], (128, 128))

    def fill_onehot(i, carry):
        first = i * 128
        row = (iota((128, 128), 0) + first).astype(F32)
        for j in range(SLOTS):
            match = jnp.where(row == rows_of[j : j + 1, :], 1.0, 0.0)
            onehot[pl.ds(pl.multiple_of(first, 128), 128), pl.ds(j * 128, 128)] = match.astype(BF16)
        return carry

    lax.fori_loop(0, CELLS // 128, fill_onehot, 0)

    def inject(dst):
        lanes = iota((128, 128), 1).astype(F32)
        for j in range(SLOTS):
            column = inc[:, j * STEPS : j * STEPS + 1]
            value = jnp.where(lanes_of[pl.ds(j * 128, 128), :] == lanes, column, 0.0)
            for i, part in enumerate(three(value)):
                rhs[pl.ds(j * 128, 128), pl.ds(i * 128, 128)] = part
        inc[...] = pltpu.roll(inc[...], 127, axis=1)

        def chunk(i, carry):
            first = pl.multiple_of(i * 512, 512)
            out = dot(onehot[pl.ds(first, 512), :], rhs[...])
            dst[pl.ds(first, 512), :] = (out[:, 0:128] + out[:, 128:256]) + out[:, 256:384]
            return carry

        lax.fori_loop(0, CELLS // 512, chunk, 0)

    inject(inj.at[0])
    inject(inj.at[1])

    for copy in loads:
        copy.wait()
    p0 = p2.at[0]

    def bring(x, carry):
        def turned(ref):
            parts = [ref[pl.ds(g * XI + x, EVENTS, stride=TILE), :] for g in range(GROUPS)]
            return jnp.concatenate(parts, axis=0).T

        def spread(ref, base, value):
            for g in range(8):
                ref[pl.ds(base + g, YI, stride=8), :] = value[g * YI : (g + 1) * YI, :]

        deep = jnp.concatenate(
            [jnp.broadcast_to(depth_ref[pl.ds(g * XI + x, 1), :], (EVENTS, TILE)) for g in range(GROUPS)],
            axis=0,
        ).T
        scaled = deep * 0.6
        spread(cf, c_row(x, 0), scaled * 0.6)
        spread(p0, p_row(x, 0), turned(stage.at[0]))
        spread(wf, w_row(x, 0), turned(stage.at[1]) * scaled)
        spread(vf, v_row(x, 0), turned(stage.at[2]) * scaled)
        for y in range(YI):
            put(p0, p_row(x, y), tile(p0, p_row(x, y)) + tile(inj.at[0], c_row(x, y)))
        return carry

    lax.fori_loop(0, XI, bring, 0)

    def send_edges(ref, slot):
        def pack(d):
            if d == 0:
                value = jnp.concatenate(pack_x(lambda y: tile(ref, p_row(XI - 1, y)), GROUPS - 1), axis=0)
            elif d == 1:
                value = jnp.concatenate(pack_x(lambda y: tile(ref, p_row(0, y)), 0), axis=0)
            elif d == 2:
                value = ref[pl.ds((YI - 1) * 8 + 7, XI, stride=PY * 8), :]
            else:
                value = ref[pl.ds(0, XI, stride=PY * 8), :]
            send_buf[d, slot] = value

        for d in range(4):
            pack(d)

            @pl.when(sends[d])
            def _():
                edge_copy(d, slot).start()

    send_edges(p0, 0)
    init_send[0, 0:32] = jnp.concatenate(pack_x(lambda y: tile(wf, w_row(XI - 1, y)), GROUPS - 1), axis=0)
    init_send[0, 32:64] = jnp.concatenate(pack_x(lambda y: tile(cf, c_row(XI - 1, y)), GROUPS - 1), axis=0)
    init_send[1, 0:32] = vf[pl.ds(v_row(0, YI - 1) + 7, XI, stride=PY * 8), :]
    init_send[1, 32:64] = cf[pl.ds(c_row(0, YI - 1) + 7, XI, stride=YI * 8), :]
    for i in range(2):

        @pl.when(sends[2 * i])
        def _():
            init_copy(i).start()

    for i in range(2):

        @pl.when(receives[2 * i])
        def _():
            init_copy(i).wait_recv()

    for y in range(YI):
        wh[pl.ds(y * 8, 8), :] = jnp.where(group == 0, unpack_x(init_recv.at[0, pl.ds(0, 32)], y, 0), 0.0)
        ch[pl.ds(y * 8, 8), :] = jnp.where(group == 0, unpack_x(init_recv.at[0, pl.ds(32, 32)], y, 0), 0.0)
    vh[...] = init_recv[1, 0:32]
    chy[...] = init_recv[1, 32:64]

    def step(now, later, last):
        pc, pn = p2.at[now], p2.at[later]
        add = None if last else inj.at[later]
        for d in range(4):

            @pl.when(receives[d])
            def _():
                edge_copy(d, now).wait_recv()

        for y in range(YI):
            own = tile(pc, p_row(0, y))
            beyond = unpack_x(recv_buf.at[1, now], y, GROUPS - 1)
            put(pc, p_row(XI, y), jnp.where(lane < 128 - EVENTS, pltpu.roll(own, 128 - EVENTS, axis=1), beyond))
            before = unpack_x(recv_buf.at[0, now], y, 0)
            rows = pl.ds(y * 8, 8)
            wh[rows, :] = wh[rows, :] - ch[rows, :] * (own - before)
        vh[...] = vh[...] - chy[...] * (pc[pl.ds(0, XI, stride=PY * 8), :] - recv_buf[2, now])
        for x in range(XI):
            beyond = jnp.broadcast_to(recv_buf[3, now, pl.ds(x, 1), :], (8, 128))
            put(pc, p_row(x, YI), jnp.where(sub < 7, pltpu.roll(tile(pc, p_row(x, 0)), 7, axis=0), beyond))

        def flow(x, columns):
            for y in columns:
                own, c = tile(pc, p_row(x, y)), tile(cf, c_row(x, y))
                put(wf, w_row(x, y), tile(wf, w_row(x, y)) - c * (tile(pc, p_row(x + 1, y)) - own))
                put(vf, v_row(x, y), tile(vf, v_row(x, y)) - c * (tile(pc, p_row(x, y + 1)) - own))

        def height(x, columns):
            for y in columns:
                out = tile(pc, p_row(x, y)) - (
                    (tile(wf, w_row(x, y)) - tile(wf, w_row(x - 1, y)))
                    + (tile(vf, v_row(x, y)) - tile(vf, v_row(x, y - 1)))
                )
                if add is not None:
                    out = out + tile(add, c_row(x, y))
                put(pn, p_row(x, y), out)

        def over(first, end, body):
            lax.fori_loop(first, end, lambda x, carry: (body(x), carry)[1], 0)

        everywhere = range(YI)
        for x in (0, XI - 2, XI - 1):
            flow(x, everywhere)
        over(1, XI - 2, lambda x: flow(x, (0, YI - 2, YI - 1)))
        for y in range(YI):
            own = tile(wf, w_row(XI - 1, y))
            put(wf, w_row(-1, y), jnp.where(group > 0, pltpu.roll(own, EVENTS, axis=1), wh[pl.ds(y * 8, 8), :]))
        for x in range(XI):
            before = jnp.broadcast_to(vh[pl.ds(x, 1), :], (8, 128))
            own = tile(vf, v_row(x, YI - 1))
            put(vf, v_row(x, -1), jnp.where(sub > 0, pltpu.roll(own, 1, axis=0), before))
        for x in (0, XI - 1):
            height(x, everywhere)
        over(1, XI - 1, lambda x: height(x, (0, YI - 1)))
        if not last:
            for d in range(4):

                @pl.when(sends[d])
                def _():
                    edge_copy(d, now).wait_send()

            send_edges(pn, later)

        def inside(x):
            flow(x, range(1, YI - 2))
            height(x, range(1, YI - 1))

        over(1, XI - 2, inside)
        height(XI - 2, range(1, YI - 1))
        if last:
            for d in range(4):

                @pl.when(sends[d])
                def _():
                    edge_copy(d, now).wait_send()

    def advance(t, carry):
        now = lax.rem(t, 2)
        step(now, 1 - now, False)
        inject(inj.at[now])
        return carry

    lax.fori_loop(0, STEPS - 1, advance, 0)
    step((STEPS - 1) % 2, STEPS % 2, True)
    for i in range(2):

        @pl.when(sends[2 * i])
        def _():
            init_copy(i).wait_send()

    stores = []
    final = p2.at[STEPS % 2]
    for i, (ref, row, out) in enumerate(((final, p_row, p_out), (wf, w_row, q_out), (vf, v_row, r_out))):

        def back(x, carry, i=i, ref=ref, row=row):
            def gathered(source, base):
                parts = [source[pl.ds(base + g, YI, stride=8), :] for g in range(8)]
                return jnp.concatenate(parts, axis=0)

            value = gathered(ref, row(x, 0))
            if i:
                value = value * (0.6 / gathered(cf, c_row(x, 0)))
            turned = value.T
            for g in range(GROUPS):
                stage[i, pl.ds(g * XI + x, EVENTS, stride=TILE), :] = turned[g * EVENTS : (g + 1) * EVENTS, :]
            return carry

        lax.fori_loop(0, XI, back, 0)
        copy = pltpu.make_async_copy(stage.at[i], out, out_sem.at[i])
        copy.start()
        stores.append(copy)
    for copy in stores:
        copy.wait()


def local(
    height_start, flow_x_start, flow_y_start, depth_field,
    misfit_rows, tile_list, member_list, cell_list, count_list,
):
    shape = height_start.shape
    meta = jnp.stack([tile_list[:, 0], member_list, cell_list, count_list])
    vmem = pl.BlockSpec(memory_space=pltpu.VMEM)
    hbm = pl.BlockSpec(memory_space=pl.ANY)
    slots = pl.pallas_call(
        slot_kernel,
        out_shape=jax.ShapeDtypeStruct((128, 256), F32),
        in_specs=[vmem, vmem],
        out_specs=vmem,
    )(misfit_rows, meta)
    slots = lax.all_to_all(slots, ("gx", "gy"), split_axis=0, concat_axis=0, tiled=True)
    field = jax.ShapeDtypeStruct((CELLS, 128), F32)
    flat = [a.reshape(CELLS, 128) for a in (height_start, flow_x_start, flow_y_start)]
    outs = pl.pallas_call(
        sweep_kernel,
        out_shape=(field, field, field),
        in_specs=[hbm, hbm, hbm, vmem, vmem],
        out_specs=(hbm, hbm, hbm),
        scratch_shapes=[
            pltpu.VMEM((3, CELLS, 128), F32),
            pltpu.VMEM((2, (XI + 1) * PY * 8, 128), F32),
            pltpu.VMEM(((XI + 1) * YI * 8, 128), F32),
            pltpu.VMEM((XI * PY * 8, 128), F32),
            pltpu.VMEM((CELLS, 128), F32),
            pltpu.VMEM((2, CELLS, 128), F32),
            pltpu.VMEM((CELLS, SLOTS * 128), BF16),
            pltpu.VMEM((SLOTS * 128, 3 * 128), BF16),
            pltpu.VMEM((SLOTS * 128, 128), F32),
            pltpu.VMEM((128, 128), F32),
            pltpu.VMEM((4, 2, 32, 128), F32),
            pltpu.VMEM((4, 2, 32, 128), F32),
            pltpu.VMEM((2, 64, 128), F32),
            pltpu.VMEM((2, 64, 128), F32),
            pltpu.VMEM((128, 128), F32),
            pltpu.VMEM((128, 128), F32),
            pltpu.VMEM((32, 128), F32),
            pltpu.VMEM((32, 128), F32),
            pltpu.SemaphoreType.DMA((3,)),
            pltpu.SemaphoreType.DMA((3,)),
            pltpu.SemaphoreType.DMA((4, 2)),
            pltpu.SemaphoreType.DMA((4, 2)),
            pltpu.SemaphoreType.DMA((2,)),
            pltpu.SemaphoreType.DMA((2,)),
        ],
        compiler_params=pltpu.CompilerParams(
            collective_id=0, has_side_effects=True, vmem_limit_bytes=48 * 1024 * 1024
        ),
    )(*flat, depth_field, slots)
    return tuple(a.reshape(shape) for a in outs)


def solution(mesh):
    in_specs = (
        P(None, "gx", "gy"),
        P(None, "gx", "gy"),
        P(None, "gx", "gy"),
        P("gx", "gy"),
        P(("gx", "gy"), None),
        P(("gx", "gy"), None),
        P(("gx", "gy")),
        P(("gx", "gy")),
        P(("gx", "gy")),
    )
    out_specs = (P(None, "gx", "gy"), P(None, "gx", "gy"), P(None, "gx", "gy"))
    return jax.shard_map(local, mesh=mesh, in_specs=in_specs, out_specs=out_specs, check_vma=False)
```

time: 1560 us -> 278 us (0.18)
  other arithmetic: 605 us -> 1.33 us
  local copies, waits for them, and re-layouts: 484 us -> 6.87 us
  starting transfers between devices: 427 us -> 0 us
  Pallas kernels: 0 us -> 249 us
  waiting for transfers between devices: 28.2 us -> 0 us
  blocking collectives: 0 us -> 18.6 us
    ppermute x128 -> x0, starting transfers between devices: 410 us -> none  [shifted(): lax.ppermute(value, axis, [(source, source + steps) for source in range(l...]
    slice x224 -> x0, local copies, waits for them, and re-layouts: 292 us -> none  [the longest x64 132 us: advance(): back_y = shifted(flux_y[:, :, -1:], 'gy', 1)]
    mul x32 -> x0, other arithmetic: 273 us -> none  [advance(): flux_y = depth * flow_y]
    pallas_call x0 -> x2, Pallas kernels: none -> 249 us  [the longest x1 246 us: local(): pl.pallas_call(sweep_kernel, out_shape=(field, field, field), in_specs=[h...]
    sub x32 -> x0, other arithmetic: 193 us -> none  [advance(): height = height - 0.6 * (flux_x - prev_x + (flux_y - prev_y))]
    scatter-add x32 -> x0, other arithmetic: 131 us -> none  [advance(): height.reshape(-1).at[flat_index].add(amounts).reshape(height.shape)]
    ppermute x64 -> x0, local copies, waits for them, and re-layouts: 126 us -> none  [shifted(): lax.ppermute(value, axis, [(source, source + steps) for source in range(l...]
    while x65 -> x0, local copies, waits for them, and re-layouts: 42.3 us -> none
  transfers between devices with their start and end apart: 130 -> 0, of which waited for: 33 -> 0; matrix products, arithmetic and copies ran while one was open for 17% -> 0% of each run, Pallas kernels for 0% -> 0%
where the time goes in v1:
time: 278 us; the launch traced here: 276 us
  Pallas kernels  249 us (90%)
  blocking collectives  18.6 us (7%)
  local copies, waits for them, and re-layouts  6.87 us (2%)
    pallas_call x1, Pallas kernels, local(): pl.pallas_call(sweep_kernel, out_shape=(field, field, field), in_specs=[h...  246 us
    all_to_all x1, blocking collectives, local(): lax.all_to_all(slots, ('gx', 'gy'), split_axis=0, concat_axis=0, tiled=True)  18.6 us
    unnamed x8, local copies, waits for them, and re-layouts  5.83 us

profile of v1, /device:TPU:24, one launch (start us, length us, event | category | flops | bytes accessed | tf_op | source)
XLA Modules:
  0.0 276.1 jit_solution(909382242912083468)
XLA Ops:
  0.6 1.3 pad_add_fusion.meta_ref
  2.0 2.6 shard_map.112
  4.5 1.0 copy.12
  5.6 18.6 %all_to_all.11 = f32[128,1,256]{2,1,0:T(1,128)S(1)} all-to-all(f32[128,1,256]{2,1,0:T(1,128)S(1)} %copy.12), channel_id=1, replica_groups=mesh['gx'=16,'gy'=8] {'gx','gy'}, dimensions={0} | all-to-all | bytes 262144 | tf_op jit(solution)/shard_map/all_to_all | solution.py:395
  24.2 0.0 copy-start
  24.2 0.8 copy-done
  25.0 246.1 %shard_map.113 = (f32[4096,128]{1,0:T(8,128)S(1)}, f32[4096,128]{1,0:T(8,128)S(1)}, f32[4096,128]{1,0:T(8,128)}) custom-call(f32[4096,128]{1,0:T(8,128)} %bitcast.17, f32[4096,128]{1,0:T(8,128)} %bitcast.18, f32[4096,128]{1,0:T(8,128)} %bitcast.19, f32[128,128]{1,0:T(8,128)S(1)} %copy-done, f32[128,256]{1,0:T(8,128)S(1)} %bitcast.16), custom_call_target="tpu_custom_call" | custom-call | tf_op jit(solution)/shard_map/pallas_call | solution.py:398
  271.1 1.3 copy.19
  272.5 0.0 copy-start.1
  272.5 1.3 copy.20
  273.8 1.0 copy-done.1
  274.8 1.3 copy.21
  (1 shorter events, 0.0 us)
Async XLA Ops:
  24.2 0.8 copy-start
  272.5 2.3 copy-start.1

commit v2 on v1

--- a/solution.py
+++ b/solution.py
@@ -17,6 +17,12 @@
 PY = YI + 1
 SLOTS = 4
 CELLS = TILE * TILE * EVENTS // 128
+TILES = CELLS // 8
+TURNS = XI - 3
+SHARE = 9
+PLACES = 640
+EMPTY = 2 * TURNS * SHARE
+MIDDLE = EMPTY + 1
 
 
 def three(x):
@@ -67,9 +73,59 @@
     out_ref[:, 128:256] = ids
 
 
+def prep_kernel(slots_ref, values_ref, keep_ref, place_ref, last_ref):
+    slots = SLOTS * 128
+    half = slots // 2
+    ids = slots_ref[:, 128:256]
+    turned = ids.T
+    rows = jnp.concatenate([ids[:, j : j + 1] for j in range(SLOTS)], axis=0).astype(jnp.int32)
+    lanes = jnp.concatenate([ids[:, SLOTS + j : SLOTS + j + 1] for j in range(SLOTS)], axis=0).astype(jnp.int32)
+    across = jnp.concatenate([turned[j : j + 1, :] for j in range(SLOTS)], axis=1).astype(jnp.int32)
+    down_tile = jnp.where(rows < 0, TILES, rows >> 3)
+    across_tile = jnp.where(across < 0, TILES, across >> 3)
+    down_key = down_tile * slots + iota((slots, 1), 0)
+    across_key = across_tile * slots + iota((1, slots), 1)
+
+    def position(rank):
+        upper = rank >= half
+        away = jnp.where(upper, slots - 1 - rank, rank)
+        turn = (away * 7282) >> 16
+        return turn * (2 * SHARE) + (away - turn * SHARE) + jnp.where(upper, SHARE, 0)
+
+    below = jnp.where(down_key < across_key, 1.0, 0.0)
+    rank = jnp.sum(below, axis=0, keepdims=True).astype(jnp.int32)
+    order = jnp.where(position(rank) == iota((PLACES, slots), 0), 1.0, 0.0).astype(BF16)
+    above = jnp.sum(below, axis=1, keepdims=True)
+    same = down_tile == across_tile
+    same_above = jnp.sum(jnp.where(same, below, 0.0), axis=1, keepdims=True)
+    same_below = jnp.sum(jnp.where(same, 1.0 - below, 0.0), axis=1, keepdims=True) - 1.0
+    in_upper = above < half
+    first_of = jnp.where(in_upper, same_above, same_below) < 0.5
+    lane = iota((slots, 128), 1)
+    increments = jnp.concatenate(
+        [slots_ref[:, 0:128]] + [pltpu.roll(slots_ref[:, 0:128], 128 - STEPS * j, axis=1) for j in range(1, SLOTS)],
+        axis=0,
+    )
+    table = jnp.where(lane < STEPS, increments, 0.0)
+    table = jnp.where(lane == STEPS, ((rows & 7) * 128 + lanes).astype(F32), table)
+    table = jnp.where(lane == STEPS + 1, jnp.where(first_of, 1.0, 0.0), table)
+    a, b, c = three(table)
+    ordered = (dot(order, a) + dot(order, b)) + dot(order, c)
+    flat = ordered.T
+    values_ref[...] = flat[0:STEPS, :]
+    place_ref[...] = flat[STEPS : STEPS + 1, :].astype(jnp.int32)
+    keep_ref[...] = 1.0 - flat[STEPS + 1 : STEPS + 2, :]
+    wanted = iota((1, TILES), 1)
+    upto = jnp.sum(jnp.where(down_tile <= wanted, 1.0, 0.0), axis=0, keepdims=True).astype(jnp.int32)
+    before = jnp.sum(jnp.where(down_tile < wanted, 1.0, 0.0), axis=0, keepdims=True).astype(jnp.int32)
+    last = upto - 1
+    where = jnp.where(last < half, position(last), jnp.where(before >= half, position(before), MIDDLE))
+    last_ref[...] = jnp.where(upto > before, where, EMPTY)
+
+
 def sweep_kernel(
-    p_in, q_in, r_in, depth_ref, slots_ref, p_out, q_out, r_out,
-    stage, p2, wf, vf, cf, inj, onehot, rhs, lanes_of, inc,
+    p_in, q_in, r_in, depth_ref, values, keeps, places, lasts, p_out, q_out, r_out,
+    stage, pa, pb, wf, vf, cf, ta, tb,
     send_buf, recv_buf, init_send, init_recv, wh, ch, vh, chy,
     in_sem, out_sem, send_sem, recv_sem, init_send_sem, init_recv_sem,
 ):
@@ -157,45 +213,30 @@
         shift = ((to - y % 4) * EVENTS) % 128
         return pltpu.roll(value, shift, axis=1) if shift else value
 
-    inc[...] = slots_ref[:, 0:128]
-    ids = slots_ref[:, 128:256]
-    rows_of = ids.T
-    for j in range(SLOTS):
-        lanes_of[pl.ds(j * 128, 128), :] = jnp.broadcast_to(ids[:, SLOTS + j : SLOTS + j + 1], (128, 128))
-
-    def fill_onehot(i, carry):
-        first = i * 128
-        row = (iota((128, 128), 0) + first).astype(F32)
-        for j in range(SLOTS):
-            match = jnp.where(row == rows_of[j : j + 1, :], 1.0, 0.0)
-            onehot[pl.ds(pl.multiple_of(first, 128), 128), pl.ds(j * 128, 128)] = match.astype(BF16)
-        return carry
-
-    lax.fori_loop(0, CELLS // 128, fill_onehot, 0)
-
-    def inject(dst):
-        lanes = iota((128, 128), 1).astype(F32)
-        for j in range(SLOTS):
-            column = inc[:, j * STEPS : j * STEPS + 1]
-            value = jnp.where(lanes_of[pl.ds(j * 128, 128), :] == lanes, column, 0.0)
-            for i, part in enumerate(three(value)):
-                rhs[pl.ds(j * 128, 128), pl.ds(i * 128, 128)] = part
-        inc[...] = pltpu.roll(inc[...], 127, axis=1)
-
-        def chunk(i, carry):
-            first = pl.multiple_of(i * 512, 512)
-            out = dot(onehot[pl.ds(first, 512), :], rhs[...])
-            dst[pl.ds(first, 512), :] = (out[:, 0:128] + out[:, 128:256]) + out[:, 256:384]
-            return carry
-
-        lax.fori_loop(0, CELLS // 512, chunk, 0)
-
-    inject(inj.at[0])
-    inject(inj.at[1])
+    place_iota = sub * 128 + lane
+
+    def gathered(table, x, y):
+        return table[lasts[x * YI + y]]
+
+    def build(table, t, turn, carry):
+        first, base = turn * (2 * SHARE), t * PLACES + turn * (2 * SHARE)
+        carry = list(carry)
+        for i in range(SHARE):
+            for side in range(2):
+                n = side * SHARE + i
+                value = jnp.where(place_iota == places[first + n], values[base + n], 0.0)
+                carry[side] = value + carry[side] * keeps[first + n]
+                table[first + n] = carry[side]
+        return tuple(carry)
+
+    zero = jnp.zeros((8, 128), F32)
+    for t, table in ((0, ta), (1, tb)):
+        table[EMPTY] = zero
+        ends = lax.fori_loop(0, TURNS, lambda i, carry: build(table, t, i, carry), (zero, zero))
+        table[MIDDLE] = ends[0] + ends[1]
 
     for copy in loads:
         copy.wait()
-    p0 = p2.at[0]
 
     def bring(x, carry):
         def turned(ref):
@@ -212,11 +253,11 @@
         ).T
         scaled = deep * 0.6
         spread(cf, c_row(x, 0), scaled * 0.6)
-        spread(p0, p_row(x, 0), turned(stage.at[0]))
+        spread(pa, p_row(x, 0), turned(stage.at[0]))
         spread(wf, w_row(x, 0), turned(stage.at[1]) * scaled)
         spread(vf, v_row(x, 0), turned(stage.at[2]) * scaled)
         for y in range(YI):
-            put(p0, p_row(x, y), tile(p0, p_row(x, y)) + tile(inj.at[0], c_row(x, y)))
+            put(pa, p_row(x, y), tile(pa, p_row(x, y)) + gathered(ta, x, y))
         return carry
 
     lax.fori_loop(0, XI, bring, 0)
@@ -240,7 +281,7 @@
             def _():
                 edge_copy(d, slot).start()
 
-    send_edges(p0, 0)
+    send_edges(pa, 0)
     init_send[0, 0:32] = jnp.concatenate(pack_x(lambda y: tile(wf, w_row(XI - 1, y)), GROUPS - 1), axis=0)
     init_send[0, 32:64] = jnp.concatenate(pack_x(lambda y: tile(cf, c_row(XI - 1, y)), GROUPS - 1), axis=0)
     init_send[1, 0:32] = vf[pl.ds(v_row(0, YI - 1) + 7, XI, stride=PY * 8), :]
@@ -263,50 +304,83 @@
     vh[...] = init_recv[1, 0:32]
     chy[...] = init_recv[1, 32:64]
 
-    def step(now, later, last):
-        pc, pn = p2.at[now], p2.at[later]
-        add = None if last else inj.at[later]
+    def step(t, slot, pc, pn, table, build_table):
+        def flow(x, y, own, right, down):
+            c = tile(cf, c_row(x, y))
+            w = tile(wf, w_row(x, y)) - c * (down - own)
+            v = tile(vf, v_row(x, y)) - c * (right - own)
+            put(wf, w_row(x, y), w)
+            put(vf, v_row(x, y), v)
+            return w, v
+
+        def flow_row(x, columns):
+            own = tile(pc, p_row(x, columns[0]))
+            for y in columns:
+                right = tile(pc, p_row(x, y + 1))
+                flow(x, y, own, right, tile(pc, p_row(x + 1, y)))
+                own = right
+
+        def flow_column(first, count, y):
+            own = tile(pc, p_row(first, y))
+            for i in range(count):
+                down = tile(pc, p_row(first + i + 1, y))
+                flow(first + i, y, own, tile(pc, p_row(first + i, y + 1)), down)
+                own = down
+
+        def height(x, y, own, w, before, v, left):
+            out = own - ((w - before) + (v - left))
+            if table is not None:
+                out = out + gathered(table, x, y)
+            put(pn, p_row(x, y), out)
+
+        def height_row(x, columns):
+            left = tile(vf, v_row(x, columns[0] - 1))
+            for y in columns:
+                v = tile(vf, v_row(x, y))
+                height(x, y, tile(pc, p_row(x, y)), tile(wf, w_row(x, y)), tile(wf, w_row(x - 1, y)), v, left)
+                left = v
+
+        def height_column(first, count, y):
+            before = tile(wf, w_row(first - 1, y))
+            for i in range(count):
+                x = first + i
+                w = tile(wf, w_row(x, y))
+                height(x, y, tile(pc, p_row(x, y)), w, before, tile(vf, v_row(x, y)), tile(vf, v_row(x, y - 1)))
+                before = w
+
+        def turns(first, size, count, body):
+            lax.fori_loop(0, count, lambda i, carry: (body(first + i * size), carry)[1], 0)
+
+        for x in (0, XI - 2):
+            flow_row(x, range(0, YI - 1))
+
+        def before_columns(first, count=7):
+            flow_column(first, count, 0)
+            flow_column(first, count, YI - 2)
+
+        turns(1, 7, 4, before_columns)
+        before_columns(XI - 3, 1)
+
         for d in range(4):
 
             @pl.when(receives[d])
             def _():
-                edge_copy(d, now).wait_recv()
+                edge_copy(d, slot).wait_recv()
 
         for y in range(YI):
             own = tile(pc, p_row(0, y))
-            beyond = unpack_x(recv_buf.at[1, now], y, GROUPS - 1)
+            beyond = unpack_x(recv_buf.at[1, slot], y, GROUPS - 1)
             put(pc, p_row(XI, y), jnp.where(lane < 128 - EVENTS, pltpu.roll(own, 128 - EVENTS, axis=1), beyond))
-            before = unpack_x(recv_buf.at[0, now], y, 0)
+            before = unpack_x(recv_buf.at[0, slot], y, 0)
             rows = pl.ds(y * 8, 8)
             wh[rows, :] = wh[rows, :] - ch[rows, :] * (own - before)
-        vh[...] = vh[...] - chy[...] * (pc[pl.ds(0, XI, stride=PY * 8), :] - recv_buf[2, now])
+        vh[...] = vh[...] - chy[...] * (pc[pl.ds(0, XI, stride=PY * 8), :] - recv_buf[2, slot])
         for x in range(XI):
-            beyond = jnp.broadcast_to(recv_buf[3, now, pl.ds(x, 1), :], (8, 128))
+            beyond = jnp.broadcast_to(recv_buf[3, slot, pl.ds(x, 1), :], (8, 128))
             put(pc, p_row(x, YI), jnp.where(sub < 7, pltpu.roll(tile(pc, p_row(x, 0)), 7, axis=0), beyond))
 
-        def flow(x, columns):
-            for y in columns:
-                own, c = tile(pc, p_row(x, y)), tile(cf, c_row(x, y))
-                put(wf, w_row(x, y), tile(wf, w_row(x, y)) - c * (tile(pc, p_row(x + 1, y)) - own))
-                put(vf, v_row(x, y), tile(vf, v_row(x, y)) - c * (tile(pc, p_row(x, y + 1)) - own))
-
-        def height(x, columns):
-            for y in columns:
-                out = tile(pc, p_row(x, y)) - (
-                    (tile(wf, w_row(x, y)) - tile(wf, w_row(x - 1, y)))
-                    + (tile(vf, v_row(x, y)) - tile(vf, v_row(x, y - 1)))
-                )
-                if add is not None:
-                    out = out + tile(add, c_row(x, y))
-                put(pn, p_row(x, y), out)
-
-        def over(first, end, body):
-            lax.fori_loop(first, end, lambda x, carry: (body(x), carry)[1], 0)
-
-        everywhere = range(YI)
-        for x in (0, XI - 2, XI - 1):
-            flow(x, everywhere)
-        over(1, XI - 2, lambda x: flow(x, (0, YI - 2, YI - 1)))
+        flow_row(XI - 1, range(YI))
+        flow_column(0, XI - 1, YI - 1)
         for y in range(YI):
             own = tile(wf, w_row(XI - 1, y))
             put(wf, w_row(-1, y), jnp.where(group > 0, pltpu.roll(own, EVENTS, axis=1), wh[pl.ds(y * 8, 8), :]))
@@ -315,38 +389,52 @@
             own = tile(vf, v_row(x, YI - 1))
             put(vf, v_row(x, -1), jnp.where(sub > 0, pltpu.roll(own, 1, axis=0), before))
         for x in (0, XI - 1):
-            height(x, everywhere)
-        over(1, XI - 1, lambda x: height(x, (0, YI - 1)))
-        if not last:
-            for d in range(4):
-
-                @pl.when(sends[d])
-                def _():
-                    edge_copy(d, now).wait_send()
-
-            send_edges(pn, later)
-
-        def inside(x):
-            flow(x, range(1, YI - 2))
-            height(x, range(1, YI - 1))
-
-        over(1, XI - 2, inside)
-        height(XI - 2, range(1, YI - 1))
-        if last:
-            for d in range(4):
-
-                @pl.when(sends[d])
-                def _():
-                    edge_copy(d, now).wait_send()
-
-    def advance(t, carry):
-        now = lax.rem(t, 2)
-        step(now, 1 - now, False)
-        inject(inj.at[now])
+            height_row(x, range(YI))
+
+        def edge_columns(first):
+            height_column(first, 6, 0)
+            height_column(first, 6, YI - 1)
+
+        turns(1, 6, 5, edge_columns)
+        for d in range(4):
+
+            @pl.when(sends[d])
+            def _():
+                edge_copy(d, slot).wait_send()
+
+        if table is not None:
+            send_edges(pn, 1 - slot)
+
+        def inside(i, carry):
+            x = i + 1
+            if build_table is not None:
+                carry = build(build_table, t + 2, i, carry)
+            own = tile(pc, p_row(x, 1))
+            left = tile(vf, v_row(x, 0))
+            for y in range(1, YI - 1):
+                if y < YI - 2:
+                    right = tile(pc, p_row(x, y + 1))
+                    w, v = flow(x, y, own, right, tile(pc, p_row(x + 1, y)))
+                else:
+                    right = None
+                    w, v = tile(wf, w_row(x, y)), tile(vf, v_row(x, y))
+                height(x, y, own, w, tile(wf, w_row(x - 1, y)), v, left)
+                own, left = right, v
+            return carry
+
+        ends = lax.fori_loop(0, TURNS, inside, (zero, zero))
+        if build_table is not None:
+            build_table[MIDDLE] = ends[0] + ends[1]
+        height_row(XI - 2, range(1, YI - 1))
+
+    def advance(i, carry):
+        step(2 * i, 0, pa, pb, tb, ta)
+        step(2 * i + 1, 1, pb, pa, ta, tb)
         return carry
 
-    lax.fori_loop(0, STEPS - 1, advance, 0)
-    step((STEPS - 1) % 2, STEPS % 2, True)
+    lax.fori_loop(0, STEPS // 2 - 1, advance, 0)
+    step(STEPS - 2, 0, pa, pb, tb, None)
+    step(STEPS - 1, 1, pb, pa, None, None)
     for i in range(2):
 
         @pl.when(sends[2 * i])
@@ -354,17 +442,16 @@
             init_copy(i).wait_send()
 
     stores = []
-    final = p2.at[STEPS % 2]
-    for i, (ref, row, out) in enumerate(((final, p_row, p_out), (wf, w_row, q_out), (vf, v_row, r_out))):
+    for i, (ref, row, out) in enumerate(((pa, p_row, p_out), (wf, w_row, q_out), (vf, v_row, r_out))):
 
         def back(x, carry, i=i, ref=ref, row=row):
-            def gathered(source, base):
+            def collected(source, base):
                 parts = [source[pl.ds(base + g, YI, stride=8), :] for g in range(8)]
                 return jnp.concatenate(parts, axis=0)
 
-            value = gathered(ref, row(x, 0))
+            value = collected(ref, row(x, 0))
             if i:
-                value = value * (0.6 / gathered(cf, c_row(x, 0)))
+                value = value * (0.6 / collected(cf, c_row(x, 0)))
             turned = value.T
             for g in range(GROUPS):
                 stage[i, pl.ds(g * XI + x, EVENTS, stride=TILE), :] = turned[g * EVENTS : (g + 1) * EVENTS, :]
@@ -393,24 +480,34 @@
         out_specs=vmem,
     )(misfit_rows, meta)
     slots = lax.all_to_all(slots, ("gx", "gy"), split_axis=0, concat_axis=0, tiled=True)
+    tables = pl.pallas_call(
+        prep_kernel,
+        out_shape=(
+            jax.ShapeDtypeStruct((STEPS, PLACES), F32),
+            jax.ShapeDtypeStruct((1, PLACES), F32),
+            jax.ShapeDtypeStruct((1, PLACES), jnp.int32),
+            jax.ShapeDtypeStruct((1, TILES), jnp.int32),
+        ),
+        in_specs=[vmem],
+        out_specs=(vmem,) * 4,
+    )(slots)
     field = jax.ShapeDtypeStruct((CELLS, 128), F32)
+    smem = pl.BlockSpec(memory_space=pltpu.SMEM)
     flat = [a.reshape(CELLS, 128) for a in (height_start, flow_x_start, flow_y_start)]
     outs = pl.pallas_call(
         sweep_kernel,
         out_shape=(field, field, field),
-        in_specs=[hbm, hbm, hbm, vmem, vmem],
+        in_specs=[hbm, hbm, hbm, vmem, smem, smem, smem, smem],
         out_specs=(hbm, hbm, hbm),
         scratch_shapes=[
             pltpu.VMEM((3, CELLS, 128), F32),
-            pltpu.VMEM((2, (XI + 1) * PY * 8, 128), F32),
+            pltpu.VMEM(((XI + 1) * PY * 8, 128), F32),
+            pltpu.VMEM(((XI + 1) * PY * 8, 128), F32),
             pltpu.VMEM(((XI + 1) * YI * 8, 128), F32),
             pltpu.VMEM((XI * PY * 8, 128), F32),
             pltpu.VMEM((CELLS, 128), F32),
-            pltpu.VMEM((2, CELLS, 128), F32),
-            pltpu.VMEM((CELLS, SLOTS * 128), BF16),
-            pltpu.VMEM((SLOTS * 128, 3 * 128), BF16),
-            pltpu.VMEM((SLOTS * 128, 128), F32),
-            pltpu.VMEM((128, 128), F32),
+            pltpu.VMEM((MIDDLE + 1, 8, 128), F32),
+            pltpu.VMEM((MIDDLE + 1, 8, 128), F32),
             pltpu.VMEM((4, 2, 32, 128), F32),
             pltpu.VMEM((4, 2, 32, 128), F32),
             pltpu.VMEM((2, 64, 128), F32),
@@ -429,7 +526,7 @@
         compiler_params=pltpu.CompilerParams(
             collective_id=0, has_side_effects=True, vmem_limit_bytes=48 * 1024 * 1024
         ),
-    )(*flat, depth_field, slots)
+    )(*flat, depth_field, *(a.reshape(-1) for a in tables))
     return tuple(a.reshape(shape) for a in outs)
 
 

time: 278 us -> 205 us (0.74)
  Pallas kernels: 249 us -> 174 us
    pallas_call x1, Pallas kernels: 246 us -> 167 us  [local(): pl.pallas_call(sweep_kernel, out_shape=(field, field, field), in_specs=[h...]
    pallas_call x0 -> x1, Pallas kernels: none -> 4.59 us  [local(): pl.pallas_call(prep_kernel, out_shape=(jax.ShapeDtypeStruct((STEPS, PLACE...]
    unnamed x8 -> x10, local copies, waits for them, and re-layouts: 5.83 us -> 7.16 us
where the time goes in v2:
time: 205 us
  Pallas kernels  174 us (85%)
  blocking collectives  18.6 us (9%)
  local copies, waits for them, and re-layouts  9.09 us (4%)
  other arithmetic  2.72 us (1%)
    pallas_call x1, Pallas kernels, local(): pl.pallas_call(sweep_kernel, out_shape=(field, field, field), in_specs=[h...  167 us
    all_to_all x1, blocking collectives, local(): lax.all_to_all(slots, ('gx', 'gy'), split_axis=0, concat_axis=0, tiled=True)  18.6 us
    unnamed x10, local copies, waits for them, and re-layouts  7.16 us
    pallas_call x1, Pallas kernels, local(): pl.pallas_call(prep_kernel, out_shape=(jax.ShapeDtypeStruct((STEPS, PLACE...  4.59 us

profile of v2, /device:TPU:24, one launch (start us, length us, event | category | flops | bytes accessed | tf_op | source)
XLA Modules:
  0.0 204.8 jit_solution(542632028705043289)
XLA Ops:
  0.6 1.3 pad_add_fusion.meta_ref
  2.0 2.6 %shard_map.112 = f32[128,256]{1,0:T(8,128)} custom-call(f32[256,128]{1,0:T(8,128)} %rows_ref.1, s32[4,256]{1,0:T(4,128)} %pad_add_fusion.meta_ref), custom_call_target="tpu_custom_call" | custom-call | tf_op jit(solution)/shard_map/pallas_call | solution.py:476
  4.5 1.0 copy.12
  5.6 18.6 %all_to_all.11 = f32[128,1,256]{2,1,0:T(1,128)S(1)} all-to-all(f32[128,1,256]{2,1,0:T(1,128)S(1)} %copy.12), channel_id=1, replica_groups=mesh['gx'=16,'gy'=8] {'gx','gy'}, dimensions={0} | all-to-all | bytes 262144 | tf_op jit(solution)/shard_map/all_to_all | solution.py:482
  24.2 0.7 copy.15
  24.8 4.6 %shard_map.113 = (f32[32,640]{1,0:T(8,128)}, f32[1,640]{1,0:T(1,128)}, s32[1,640]{1,0:T(1,128)}, s32[1,512]{1,0:T(1,128)}) custom-call(f32[128,256]{1,0:T(8,128)} %bitcast.22), custom_call_target="tpu_custom_call" | custom-call | tf_op jit(solution)/shard_map/pallas_call | solution.py:483
  29.4 0.9 reshape.41.values
  30.3 0.7 reduce.keeps
  31.0 0.7 reduce.1.places
  31.7 0.0 copy-start
  31.7 0.8 copy-done
  32.6 0.0 copy-start.1
  32.6 0.7 copy-done.1
  33.2 166.5 %shard_map.114 = (f32[4096,128]{1,0:T(8,128)S(1)}, f32[4096,128]{1,0:T(8,128)S(1)}, f32[4096,128]{1,0:T(8,128)}) custom-call(f32[4096,128]{1,0:T(8,128)} %bitcast.18, f32[4096,128]{1,0:T(8,128)} %bitcast.19, f32[4096,128]{1,0:T(8,128)} %bitcast.20, f32[128,128]{1,0:T(8,128)S(1)} %copy-done, f32[20480]{0:T(1024)S(1)} %reshape.41.values, f32[640]{0:T(1024)S(1)} %reduce.keeps, ...), custom_call_target="tpu_custom_call" | custom-call | tf_op jit(solution)/shard_map/pallas_call | solution.py:497
  199.8 1.3 copy.19
  201.1 0.0 copy-start.2
  201.1 1.3 copy.20
  202.4 1.0 copy-done.2
  203.5 1.3 copy.21
Async XLA Ops:
  31.7 0.8 copy-start
  32.6 0.7 copy-start.1
  201.1 2.3 %copy-start.2 = (f32[4096,128]{1,0:T(8,128)S(1)}, f32[4096,128]{1,0:T(8,128)}, u32[]{:S(2)}) copy-start(f32[4096,128]{1,0:T(8,128)} %get-tuple-element.16) | copy-start | bytes 6291460

commit v3 on v2

--- a/solution.py
+++ b/solution.py
@@ -361,12 +361,34 @@
         turns(1, 7, 4, before_columns)
         before_columns(XI - 3, 1)
 
-        for d in range(4):
-
-            @pl.when(receives[d])
-            def _():
-                edge_copy(d, slot).wait_recv()
-
+        def arrive(directions):
+            for d in directions:
+
+                @pl.when(receives[d])
+                def _():
+                    edge_copy(d, slot).wait_recv()
+
+        def beyond_left(x):
+            before = jnp.broadcast_to(vh[pl.ds(x, 1), :], (8, 128))
+            own = tile(vf, v_row(x, YI - 1))
+            put(vf, v_row(x, -1), jnp.where(sub > 0, pltpu.roll(own, 1, axis=0), before))
+
+        arrive((2, 3))
+        vh[...] = vh[...] - chy[...] * (pc[pl.ds(0, XI, stride=PY * 8), :] - recv_buf[2, slot])
+        for x in range(XI):
+            beyond = jnp.broadcast_to(recv_buf[3, slot, pl.ds(x, 1), :], (8, 128))
+            put(pc, p_row(x, YI), jnp.where(sub < 7, pltpu.roll(tile(pc, p_row(x, 0)), 7, axis=0), beyond))
+        flow_column(0, XI - 1, YI - 1)
+        for x in range(XI - 1):
+            beyond_left(x)
+
+        def edge_columns(first):
+            height_column(first, 6, 0)
+            height_column(first, 6, YI - 1)
+
+        turns(1, 6, 5, edge_columns)
+
+        arrive((0, 1))
         for y in range(YI):
             own = tile(pc, p_row(0, y))
             beyond = unpack_x(recv_buf.at[1, slot], y, GROUPS - 1)
@@ -374,28 +396,13 @@
             before = unpack_x(recv_buf.at[0, slot], y, 0)
             rows = pl.ds(y * 8, 8)
             wh[rows, :] = wh[rows, :] - ch[rows, :] * (own - before)
-        vh[...] = vh[...] - chy[...] * (pc[pl.ds(0, XI, stride=PY * 8), :] - recv_buf[2, slot])
-        for x in range(XI):
-            beyond = jnp.broadcast_to(recv_buf[3, slot, pl.ds(x, 1), :], (8, 128))
-            put(pc, p_row(x, YI), jnp.where(sub < 7, pltpu.roll(tile(pc, p_row(x, 0)), 7, axis=0), beyond))
-
         flow_row(XI - 1, range(YI))
-        flow_column(0, XI - 1, YI - 1)
         for y in range(YI):
             own = tile(wf, w_row(XI - 1, y))
             put(wf, w_row(-1, y), jnp.where(group > 0, pltpu.roll(own, EVENTS, axis=1), wh[pl.ds(y * 8, 8), :]))
-        for x in range(XI):
-            before = jnp.broadcast_to(vh[pl.ds(x, 1), :], (8, 128))
-            own = tile(vf, v_row(x, YI - 1))
-            put(vf, v_row(x, -1), jnp.where(sub > 0, pltpu.roll(own, 1, axis=0), before))
+        beyond_left(XI - 1)
         for x in (0, XI - 1):
             height_row(x, range(YI))
-
-        def edge_columns(first):
-            height_column(first, 6, 0)
-            height_column(first, 6, YI - 1)
-
-        turns(1, 6, 5, edge_columns)
         for d in range(4):
 
             @pl.when(sends[d])

time: 205 us -> 202 us (0.985)
  Pallas kernels: 174 us -> 170 us
    pallas_call x1, Pallas kernels: 167 us -> 163 us  [local(): pl.pallas_call(sweep_kernel, out_shape=(field, field, field), in_specs=[h...]
where the time goes in v3:
time: 202 us; the launch traced here: 201 us
  Pallas kernels  170 us (84%)
  blocking collectives  18.6 us (9%)
  local copies, waits for them, and re-layouts  9.09 us (4%)
  other arithmetic  2.72 us (1%)
    pallas_call x1, Pallas kernels, local(): pl.pallas_call(sweep_kernel, out_shape=(field, field, field), in_specs=[h...  163 us
    all_to_all x1, blocking collectives, local(): lax.all_to_all(slots, ('gx', 'gy'), split_axis=0, concat_axis=0, tiled=True)  18.6 us
    unnamed x10, local copies, waits for them, and re-layouts  7.16 us
    pallas_call x1, Pallas kernels, local(): pl.pallas_call(prep_kernel, out_shape=(jax.ShapeDtypeStruct((STEPS, PLACE...  4.59 us

profile of v3, /device:TPU:24, one launch (start us, length us, event | category | flops | bytes accessed | tf_op | source)
XLA Modules:
  0.0 201.1 jit_solution(7323904156021712208)
XLA Ops:
  0.6 1.3 pad_add_fusion.meta_ref
  2.0 2.6 %shard_map.112 = f32[128,256]{1,0:T(8,128)} custom-call(f32[256,128]{1,0:T(8,128)} %rows_ref.1, s32[4,256]{1,0:T(4,128)} %pad_add_fusion.meta_ref), custom_call_target="tpu_custom_call" | custom-call | tf_op jit(solution)/shard_map/pallas_call | solution.py:483
  4.5 1.0 copy.12
  5.6 18.6 %all_to_all.11 = f32[128,1,256]{2,1,0:T(1,128)S(1)} all-to-all(f32[128,1,256]{2,1,0:T(1,128)S(1)} %copy.12), channel_id=1, replica_groups=mesh['gx'=16,'gy'=8] {'gx','gy'}, dimensions={0} | all-to-all | bytes 262144 | tf_op jit(solution)/shard_map/all_to_all | solution.py:489
  24.2 0.7 copy.15
  24.8 4.6 %shard_map.113 = (f32[32,640]{1,0:T(8,128)}, f32[1,640]{1,0:T(1,128)}, s32[1,640]{1,0:T(1,128)}, s32[1,512]{1,0:T(1,128)}) custom-call(f32[128,256]{1,0:T(8,128)} %bitcast.22), custom_call_target="tpu_custom_call" | custom-call | tf_op jit(solution)/shard_map/pallas_call | solution.py:490
  29.4 0.9 reshape.41.values
  30.3 0.7 reduce.keeps
  31.0 0.7 reduce.1.places
  31.7 0.0 copy-start
  31.7 0.8 copy-done
  32.6 0.0 copy-start.1
  32.6 0.7 copy-done.1
  33.2 162.9 %shard_map.114 = (f32[4096,128]{1,0:T(8,128)S(1)}, f32[4096,128]{1,0:T(8,128)S(1)}, f32[4096,128]{1,0:T(8,128)}) custom-call(f32[4096,128]{1,0:T(8,128)} %bitcast.18, f32[4096,128]{1,0:T(8,128)} %bitcast.19, f32[4096,128]{1,0:T(8,128)} %bitcast.20, f32[128,128]{1,0:T(8,128)S(1)} %copy-done, f32[20480]{0:T(1024)S(1)} %reshape.41.values, f32[640]{0:T(1024)S(1)} %reduce.keeps, ...), custom_call_target="tpu_custom_call" | custom-call | tf_op jit(solution)/shard_map/pallas_call | solution.py:504
  196.1 1.3 copy.19
  197.5 0.0 copy-start.2
  197.5 1.3 copy.20
  198.8 1.0 copy-done.2
  199.8 1.3 copy.21
Async XLA Ops:
  31.7 0.8 copy-start
  32.6 0.7 copy-start.1
  197.5 2.3 %copy-start.2 = (f32[4096,128]{1,0:T(8,128)S(1)}, f32[4096,128]{1,0:T(8,128)}, u32[]{:S(2)}) copy-start(f32[4096,128]{1,0:T(8,128)} %get-tuple-element.16) | copy-start | bytes 6291460
